TPU v7x, 256 devices: a whole 4x4x8 slice. The times are simulated.
256 devices in a mesh: sect: 64 (over z, y, core), tp: 4 (over x).
Axes of the slice: x: 4, y: 4, z: 8, core: 2. Of those that a mesh axis runs over, the one named last changes fastest.
Arguments:
- item_hidden: bfloat16 [4096, 4096], P('sect', 'tp'), may hold values from -40 to 40
- item_gain: bfloat16 [4096], P('tp'), may hold values from 0.25 to 1.75
- send_item: int32 [64, 64, 4], P('sect'), may hold values from -1 to 63, as said below
- pos_slot: int32 [256, 192], P('sect'), may hold values from 0 to 255, as said below
- hist_len: int32 [256], P('sect'), may hold values from 64 to 128, as said below
- user_gain: bfloat16 [4096], P('tp'), may hold values from 0.25 to 1.75
- query_weight: bfloat16 [4096, 4096], P('tp', 'sect'), may hold values from -0.09375 to 0.09375
Outputs:
- item_grad: float32 [4096, 4096], P('sect', 'tp')
- user_loss: float32 [256], P('sect')
Inputs may be any that keep to these rules, and one draw needn't show every extreme that they name: `send_item`: entry [o, r, s] names item o * 64 + value, owned by device o and sent to reader r, or is -1 for an empty slot. Within one (o, r) block the named items are distinct and the filled slots come first; at least half of the 4 slots (rounded down, and at least one) are filled. In every draw some reader gets 4 filled slots from every owner. `pos_slot`: entry [u, j] names a filled slot of the buffer of the device holding user u, in the order o * 4 + s; every filled slot is named by some candidate or some history position below that user's length. `hist_len`: every device's block of 4 users holds a user of length 128.
All inputs are finite; a program needn't handle non-finite values.
Results may differ from a plain program's by a relative error of at most 0.015.
Values may be sent and summed in bfloat16 or wider, within the bound.
A program may use at most 128 MiB of HBM per device.

v0:
```python
import jax
import jax.numpy as jnp
from jax import lax
from jax.sharding import PartitionSpec as P

D = 4096
HD = 128
CAND = 64
NORM_FLOOR = 1e-06
LOGIT_SOFTNESS = 20.0


def head_norm(values, head_count):
    shaped = values.reshape(values.shape[:-1] + (head_count, values.shape[-1] // head_count))
    return shaped * lax.rsqrt(jnp.mean(shaped * shaped, axis=-1, keepdims=True) + NORM_FLOOR)


def causal_mask(lengths, history_span):
    position = jnp.arange(history_span)
    allowed = (position[None, :] <= position[:, None])[None] & (
        position[None, None, :] < lengths[:, None, None]
    )
    return allowed.astype(jnp.float32)


def attend(query_rows, normed_rows, attend_mask):
    head_count = query_rows.shape[-1] // HD
    query_heads = head_norm(query_rows, head_count).astype(jnp.bfloat16)
    key_heads = head_norm(normed_rows, head_count).astype(jnp.bfloat16)
    value_heads = normed_rows.astype(jnp.bfloat16).reshape(query_heads.shape)
    scores = jnp.einsum(
        "uihd,ujhd->uhij", query_heads, key_heads, preferred_element_type=jnp.float32
    ) * HD ** (-0.5)
    weights = jnp.exp(scores) * attend_mask[:, None]
    weights = weights / jnp.sum(weights, axis=-1, keepdims=True)
    mixed_rows = jnp.einsum(
        "uhij,ujhd->uihd",
        weights.astype(jnp.bfloat16),
        value_heads,
        preferred_element_type=jnp.float32,
    )
    return mixed_rows.reshape(query_rows.shape)


def score_parts(mixed_rows, history_rows, cand_rows):
    outputs = history_rows + mixed_rows
    follow = jnp.concatenate([history_rows[:, 1:], jnp.zeros_like(history_rows[:, :1])], axis=1)
    own_squares = jnp.sum(outputs * outputs, axis=-1)
    positive_dot_products = jnp.sum(outputs * follow, axis=-1)
    negative_dot_products = jnp.einsum(
        "uif,ucf->uic", outputs, cand_rows, precision=lax.Precision.HIGHEST
    )
    return (own_squares, positive_dot_products, negative_dot_products)


def user_losses(
    own_squares,
    positive_dot_products,
    negative_dot_products,
    next_item_square_sums,
    candidate_square_sums,
    lengths,
):
    reciprocal_norm = lax.rsqrt(own_squares + NORM_FLOOR)
    positive_target_logit = (
        LOGIT_SOFTNESS
        * positive_dot_products
        * reciprocal_norm
        * lax.rsqrt(next_item_square_sums + NORM_FLOOR)
    )
    negative_score_logits = (
        LOGIT_SOFTNESS
        * negative_dot_products
        * reciprocal_norm[..., None]
        * lax.rsqrt(candidate_square_sums + NORM_FLOOR)[:, None, :]
    )
    partition = jnp.exp(positive_target_logit) + jnp.sum(jnp.exp(negative_score_logits), axis=-1)
    terms = jnp.log(partition) - positive_target_logit
    position = jnp.arange(own_squares.shape[1])
    allowed = position[None, :] < lengths[:, None] - 1
    return jnp.sum(jnp.where(allowed, terms, 0.0), axis=-1) / (lengths - 1).astype(jnp.float32)


def slot_norm(slot_rows, slot_squares, gain_row):
    return slot_rows * lax.rsqrt(slot_squares / D + NORM_FLOOR)[:, None] * gain_row


def segment_rows(values, places, count):
    return jax.ops.segment_sum(
        values.reshape((-1,) + values.shape[2:]), places.reshape(-1), num_segments=count
    )


def local(item_hidden, item_gain, send_item, pos_slot, hist_len, user_gain, query_weight):
    hidden = item_hidden.astype(jnp.float32)
    item_squares = lax.psum(jnp.sum(hidden * hidden, axis=1), "tp")
    embedded = (
        hidden * lax.rsqrt(item_squares / D + NORM_FLOOR)[:, None] * item_gain.astype(jnp.float32)
    ).astype(jnp.bfloat16)
    send_slots = send_item[0]
    vacant = send_slots < 0
    picked = jnp.take(embedded, jnp.where(vacant, 0, send_slots), axis=0)
    outgoing = jnp.where(vacant[..., None], jnp.zeros((), jnp.bfloat16), picked)
    arrived = lax.all_to_all(outgoing, "sect", split_axis=0, concat_axis=0, tiled=True)
    feature_count = arrived.shape[-1]
    slot_rows = arrived.reshape(-1, feature_count).astype(jnp.float32)
    slot_count = slot_rows.shape[0]
    slot_squares = lax.psum(jnp.sum(slot_rows * slot_rows, axis=1), "tp")
    gain_row = user_gain.astype(jnp.float32)

    def norm_only(rows_in, squares_in):
        return slot_norm(rows_in, squares_in, gain_row)

    normed_slots, norm_back = jax.vjp(norm_only, slot_rows, slot_squares)
    normed_low = normed_slots.astype(jnp.bfloat16)
    partial_query = jnp.dot(
        normed_low,
        lax.all_gather(query_weight, "sect", axis=1, tiled=True),
        preferred_element_type=jnp.float32,
    )
    query_slots = lax.psum_scatter(
        partial_query.astype(jnp.bfloat16), "tp", scatter_dimension=1, tiled=True
    ).astype(jnp.float32)
    history_span = pos_slot.shape[1] - CAND
    hist_places = pos_slot[:, :history_span]
    cand_places = pos_slot[:, history_span:]
    follow_places = jnp.concatenate([hist_places[:, 1:], hist_places[:, :1]], axis=1)
    history_rows = slot_rows[hist_places]
    cand_rows = slot_rows[cand_places]
    normed_rows = normed_low[hist_places].astype(jnp.float32)
    query_rows = query_slots[hist_places]
    attend_mask = causal_mask(hist_len, history_span)

    def attend_only(query_in, normed_in):
        return attend(query_in, normed_in, attend_mask)

    mixed_rows, attend_back = jax.vjp(attend_only, query_rows, normed_rows)
    partial_stats, parts_back = jax.vjp(score_parts, mixed_rows, history_rows, cand_rows)
    own_squares, positive_dot_products, negative_dot_products = (
        lax.psum(partial_stats[0].astype(jnp.bfloat16), "tp").astype(jnp.float32),
        lax.psum(partial_stats[1].astype(jnp.bfloat16), "tp").astype(jnp.float32),
        lax.psum(partial_stats[2].astype(jnp.bfloat16), "tp").astype(jnp.float32),
    )
    next_item_square_sums = slot_squares[follow_places]
    candidate_square_sums = slot_squares[cand_places]

    def loss_only(own_in, hit_in, neg_in, follow_in, cand_in):
        return user_losses(own_in, hit_in, neg_in, follow_in, cand_in, hist_len)

    losses, loss_back = jax.vjp(
        loss_only,
        own_squares,
        positive_dot_products,
        negative_dot_products,
        next_item_square_sums,
        candidate_square_sums,
    )
    grad_own, grad_hit, grad_neg, grad_follow, grad_cand = loss_back(
        jnp.full(losses.shape, float(D), jnp.float32)
    )
    grad_mixed, grad_history, grad_cands = parts_back((grad_own, grad_hit, grad_neg))
    grad_query, grad_normed = attend_back(grad_mixed)
    grad_slots = segment_rows(grad_history, hist_places, slot_count) + segment_rows(
        grad_cands, cand_places, slot_count
    )
    grad_squares = segment_rows(grad_follow, follow_places, slot_count) + segment_rows(
        grad_cand, cand_places, slot_count
    )
    grad_norm_slots = segment_rows(grad_normed, hist_places, slot_count)
    grad_query_slots = segment_rows(grad_query, hist_places, slot_count)
    every_query = lax.all_gather(grad_query_slots.astype(jnp.bfloat16), "tp", axis=1, tiled=True)
    grad_from_query = lax.dot_general(
        every_query,
        lax.all_gather(query_weight, "sect", axis=1, tiled=True),
        (((1,), (1,)), ((), ())),
        preferred_element_type=jnp.float32,
    )
    grad_norm_slots = grad_norm_slots + grad_from_query
    back_rows, back_squares = norm_back(grad_norm_slots)
    back_squares = lax.psum(back_squares, "tp")
    grad_slots = grad_slots + back_rows + 2.0 * slot_rows * (grad_squares + back_squares)[:, None]
    returned = lax.all_to_all(
        grad_slots.reshape(arrived.shape).astype(jnp.bfloat16),
        "sect",
        split_axis=0,
        concat_axis=0,
        tiled=True,
    ).astype(jnp.float32)
    item_count = embedded.shape[0]
    targets = jnp.where(vacant, item_count, send_slots).reshape(-1)
    item_grad = jax.ops.segment_sum(
        returned.reshape(-1, feature_count), targets, num_segments=item_count + 1
    )[:item_count]
    return (item_grad, losses)


def solution(mesh):
    placed = (
        P("sect", "tp"),
        P("tp"),
        P("sect", None, None),
        P("sect", None),
        P("sect"),
        P("tp"),
        P("tp", "sect"),
    )
    return jax.shard_map(
        local, mesh=mesh, in_specs=placed, out_specs=(P("sect", "tp"), P("sect")), check_vma=False
    )
```

profile of v0, /device:TPU:1, one launch (start us, length us, event | category | flops | bytes accessed | tf_op | source)
XLA Modules:
  0.0 333.5 jit_solution(12200618832667628850)
XLA Ops:
  11.4 9.3 %psum.42 = f32[64]{0:T(128)S(1)} all-reduce(f32[64]{0:T(128)S(1)} %fusion.29), channel_id=1, replica_groups=mesh['sect'=64,'tp'=4] {'tp'}, use_global_device_ids=true, to_apply=%region_1.0 | all-reduce | flops 64 | bytes 512 | tf_op jit(solution)/shard_map/psum | solution.py:96
  24.4 14.3 %all-to-all-start = ((bf16[64,4,1024]{2,1,0:T(4,128)(2,1)}), bf16[64,4,1024]{2,1,0:T(4,128)(2,1)S(1)}, u32[]{:S(2)}, u32[]{:S(2)}) async-start(bf16[64,4,1024]{2,1,0:T(4,128)(2,1)} %select_select_fusion), calls=%async_computation | async-start | bytes 1048576 | tf_op jit(solution)/shard_map/all_to_all | solution.py:104
  38.9 19.4 %all-to-all-done = bf16[64,4,1024]{2,1,0:T(4,128)(2,1)S(1)} async-done(((bf16[64,4,1024]{2,1,0:T(4,128)(2,1)}), bf16[64,4,1024]{2,1,0:T(4,128)(2,1)S(1)}, u32[]{:S(2)}, u32[]{:S(2)}) %all-to-all-start) | async-done | bytes 524320 | tf_op jit(solution)/shard_map/all_to_all | solution.py:104
  58.9 6.0 %psum.43 = f32[256]{0:T(256)S(1)} all-reduce(f32[256]{0:T(256)S(1)} %reduce_sum.141), channel_id=1, replica_groups=mesh['sect'=64,'tp'=4] {'tp'}, use_global_device_ids=true, to_apply=%region_3.4 | all-reduce | flops 256 | bytes 2048 | tf_op jit(solution)/shard_map/psum | solution.py:108
  65.1 34.8 %all-gather.3.cloned.1.call-done = bf16[1024,4096]{0,1:T(8,128)(2,1)} async-done(((bf16[1024,64]{0,1:T(8,128)(2,1)}), bf16[1024,4096]{0,1:T(8,128)(2,1)}) %all-gather.3.cloned.1.call-update) | async-done | bytes 8388624 | tf_op jit(solution)/shard_map/all_gather | solution.py:118
  99.9 7.2 %convolution_convert_fusion = bf16[256,4096]{1,0:T(8,128)(2,1)} fusion(bf16[256,1024]{1,0:T(8,128)(2,1)S(1)} %multiply_convert_fusion.1, bf16[1024,4096]{0,1:T(8,128)(2,1)} %all-gather.3.cloned.1.call-done), kind=kOutput, calls=%fused_computation.14 | convolution fusion | flops 2148532224 | bytes 11010048 | tf_op jit(solution)/shard_map/dot_general | solution.py:116
  111.9 1.9 gather_fusion.6
  113.9 2.8 gather_fusion.2
  116.7 2.5 copy.131
  119.2 2.4 copy.110
  121.6 2.7 gather_fusion.1
  124.3 3.4 %copy.133 = f32[64,8,8,128]{3,2,1,0:T(8,128)} copy(f32[64,8,8,128]{3,1,2,0:T(8,128)} %bitcast.107) | data formatting | bytes 4194304
  127.6 3.1 copy.113
  130.8 1.6 slice.40
  132.5 3.5 %gather_fusion.4 = f32[512]{0:T(512)S(1)} fusion(f32[256]{0:T(256)S(1)} %psum.43, s32[1024]{0:T(1024)S(1)} %pad_clamp_fusion.1), kind=kCustom, calls=%fused_computation.4 | custom fusion | bytes 6144 | tf_op jit(solution)/shard_map/gather | solution.py:144
  137.4 2.7 gather_fusion.3
  140.1 2.1 copy.132
  144.6 1.9 copy.106
  146.6 2.8 fusion.20
  150.9 1.9 copy.112
  152.8 3.2 multiply_reduce_fusion
  156.0 2.0 convolution_convert_fusion.5
  158.1 8.6 %all-reduce.2 = (bf16[4,128]{1,0:T(4,128)(2,1)S(1)}, bf16[4,128]{1,0:T(4,128)(2,1)S(1)}) all-reduce(bf16[4,128]{1,0:T(4,128)(2,1)S(1)} %get-tuple-element.27, bf16[4,128]{1,0:T(4,128)(2,1)S(1)} %get-tuple-element.10), channel_id=1, replica_groups=mesh['sect'=64,'tp'=4] {'tp'}, use_global_device_ids=true, to_apply=%region_11.12 | all-reduce | flops 1024 | bytes 4096 | tf_op jit(solution)/shard_map/psum | solution.py:140
  167.3 34.6 %all-reduce.5.cloned.1.call-done = bf16[4,128,64]{1,2,0:T(8,128)(2,1)} async-done(((bf16[4,128,64]{1,2,0:T(8,128)(2,1)}), bf16[4,128,64]{1,2,0:T(8,128)(2,1)}) %all-reduce.5.cloned.1.call-update) | async-done | bytes 65552 | tf_op jit(solution)/shard_map/psum | solution.py:142
  205.9 3.5 %pad_add_fusion = (f32[4,128,1024]{2,1,0:T(8,128)}, bf16[4,128,1024]{2,1,0:T(8,128)(2,1)}) fusion(f32[4,127,1024]{2,1,0:T(8,128)S(1)} %slice_multiply_fusion, f32[4,128,1024]{2,1,0:T(8,128)S(1)} %get-tuple-element.11, f32[4,128]{1,0:T(4,128)S(1)} %multiply_multiply_fusion.5, f32[4,127,1024]{2,1,0:T(8,128)S(1)} %copy-done.3, ...), kind=kOutput, calls=%fused_computation.48 | convolution fusion | flops 406552576 | bytes 10005504 | tf_op jit(solution)/shard_map/transpose(jvp(uif,ucf->uic))/dot_general | solution.py:50
  209.3 2.3 copy.130
  211.6 3.2 fusion.5
  216.6 1.9 add_add_fusion.1
  218.5 2.9 copy.120
  221.4 7.5 %scatter_custom_fusion.2 = f32[256,1024]{1,0:T(8,128)} fusion(s32[512]{0:T(512)} %get-tuple-element.20, f32[64,8,8,128]{3,2,1,0:T(8,128)} %bitcast.114, f32[]{:T(128)} %constant.17.clone.1), kind=kCustom, calls=%fused_computation.37 | custom fusion | flops 524288 | bytes 3146240 | tf_op jit(solution)/shard_map/scatter-add | solution.py:89
  228.9 2.1 convert_element_type.143
  231.2 4.3 %fusion.9 = (f32[4,128,8]{1,2,0:T(8,128)S(1)}, bf16[4,8,128,128]{2,3,1,0:T(8,128)(2,1)S(1)}) fusion(bf16[4,128,8,128]{1,3,2,0:T(8,128)(2,1)} %copy.110, f32[4,128,8,128]{1,3,2,0:T(8,128)} %copy-done.1, f32[4,128,8]{1,2,0:T(8,128)S(1)} %get-tuple-element.37, bf16[4,8,128,128]{2,3,1,0:T(8,128)(2,1)} %copy-done.17, f32[4,8,128,128]{2,3,1,0:T(8,128)} %copy-done.9, ...), kind=kOutput, calls=%fused_computation.33 | convolution fusion | flops 141553664 | bytes 7667712 | tf_op jit(solution)/shard_map/transpose(jvp(uihd,ujhd->uhij))/dot_general | solution.py:31
  235.5 2.4 fusion.6
  237.9 3.0 copy.123
  241.0 2.3 scatter_custom_fusion.5
  243.3 2.3 fusion.43
  245.6 4.4 %scatter_custom_fusion.1 = f32[256,1024]{1,0:T(8,128)} fusion(s32[256]{0:T(256)S(1)} %reshape.374, f32[256,1024]{1,0:T(8,128)} %bitcast.124, f32[]{:T(128)} %constant.17.clone.1), kind=kCustom, calls=%fused_computation.68 | custom fusion | flops 262144 | bytes 1049088 | tf_op jit(solution)/shard_map/scatter-add | solution.py:89
  250.0 6.8 %scatter_custom_fusion = f32[256,1024]{1,0:T(8,128)} fusion(s32[512]{0:T(512)} %get-tuple-element.20, f32[512,1024]{1,0:T(8,128)} %bitcast.123, f32[]{:T(128)} %constant.17.clone.1), kind=kCustom, calls=%fused_computation.70 | custom fusion | flops 524288 | bytes 1049088 | tf_op jit(solution)/shard_map/scatter-add | solution.py:89
  256.8 4.2 %scatter_custom_fusion.4 = f32[256]{0:T(256)S(1)} fusion(s32[512]{0:T(512)S(1)} %add_bitcast_fusion, f32[512]{0:T(512)} %get-tuple-element.6, f32[]{:T(128)} %constant.17.clone.1), kind=kCustom, calls=%fused_computation.158 | custom fusion | flops 512 | bytes 1536 | tf_op jit(solution)/shard_map/scatter-add | solution.py:89
  261.1 5.7 %all-gather.5.cloned.1.call-done = bf16[256,4096]{1,0:T(8,128)(2,1)} async-done(((bf16[256,1024]{1,0:T(8,128)(2,1)}), bf16[256,4096]{1,0:T(8,128)(2,1)}) %all-gather.5.cloned.1.call-update) | async-done | bytes 2097168 | tf_op jit(solution)/shard_map/all_gather | solution.py:171
  266.8 7.4 %fusion.78 = f32[256,1024]{1,0:T(8,128)} fusion(bf16[256,4096]{1,0:T(8,128)(2,1)} %all-gather.5.cloned.1.call-done, bf16[1024,4096]{0,1:T(8,128)(2,1)} %all-gather.3.cloned.1.call-done), kind=kOutput, calls=%fused_computation.172 | convolution fusion | flops 2147483648 | bytes 11534336 | tf_op jit(solution)/shard_map/dot_general | solution.py:172
  274.2 7.4 %scatter_custom_fusion.3 = f32[256,1024]{1,0:T(8,128)} fusion(f32[256,1024]{1,0:T(8,128)} %fusion.78, s32[512]{0:T(512)} %get-tuple-element.20, f32[64,8,8,128]{3,2,1,0:T(8,128)S(1)} %bitcast.113), kind=kCustom, calls=%fused_computation.34 | custom fusion | flops 524288 | bytes 3145728 | tf_op jit(solution)/shard_map/scatter-add | solution.py:89
  281.6 1.5 multiply_reduce_fusion.2
  283.1 6.6 %psum.47 = f32[256]{0:T(256)S(1)} all-reduce(f32[256]{0:T(256)S(1)} %multiply_multiply_fusion.7), channel_id=1, replica_groups=mesh['sect'=64,'tp'=4] {'tp'}, use_global_device_ids=true, to_apply=%region_26.27 | all-reduce | flops 256 | bytes 2048 | tf_op jit(solution)/shard_map/psum | solution.py:180
  289.7 1.9 add_convert_fusion
  292.7 12.9 %all-to-all-start.1 = ((bf16[64,4,1024]{2,1,0:T(4,128)(2,1)}), bf16[64,4,1024]{2,1,0:T(4,128)(2,1)S(1)}, u32[]{:S(2)}, u32[]{:S(2)}) async-start(bf16[64,4,1024]{2,1,0:T(4,128)(2,1)} %convert_element_type.151), calls=%async_computation.2 | async-start | bytes 1048576 | tf_op jit(solution)/shard_map/all_to_all | solution.py:182
  306.3 16.9 %all-to-all-done.1 = bf16[64,4,1024]{2,1,0:T(4,128)(2,1)S(1)} async-done(((bf16[64,4,1024]{2,1,0:T(4,128)(2,1)}), bf16[64,4,1024]{2,1,0:T(4,128)(2,1)S(1)}, u32[]{:S(2)}, u32[]{:S(2)}) %all-to-all-start.1) | async-done | bytes 524320 | tf_op jit(solution)/shard_map/all_to_all | solution.py:182
  323.3 2.7 scatter_custom_fusion.6
  (164 shorter events, 28.0 us)
Async XLA Ops:
  7.2 92.7 %all-gather.3.cloned.1.call-start = ((), (), s32[]{:S(2)}) async-start(), calls=%async_computation.3 | async-start | bytes 8519680 | tf_op jit(solution)/shard_map/all_gather | solution.py:118
  22.9 15.9 %copy-start.39 = (bf16[1024]{0:T(1024)(128)(2,1)S(1)}, bf16[1024]{0:T(1024)(128)(2,1)}, u32[]{:S(2)}) copy-start(bf16[1024]{0:T(1024)(128)(2,1)} %param.12) | copy-start | bytes 6148
  24.4 33.8 %all-to-all-start = ((bf16[64,4,1024]{2,1,0:T(4,128)(2,1)}), bf16[64,4,1024]{2,1,0:T(4,128)(2,1)S(1)}, u32[]{:S(2)}, u32[]{:S(2)}) async-start(bf16[64,4,1024]{2,1,0:T(4,128)(2,1)} %select_select_fusion), calls=%async_computation | async-start | bytes 1048576 | tf_op jit(solution)/shard_map/all_to_all | solution.py:104
  38.8 97.4 %reduce-scatter.2.cloned.1.call-start = ((), (), s32[]{:S(2)}) async-start(), calls=%async_computation.4 | async-start | bytes 2621440 | tf_op jit(solution)/shard_map/reduce_scatter | solution.py:121
  64.9 35.0 %copy-start.31 = (f32[256]{0:T(256)}, f32[256]{0:T(256)S(1)}, u32[]{:S(2)}) copy-start(f32[256]{0:T(256)S(1)} %fusion.65) | copy-start | bytes 3076
  107.1 3.3 copy-start.41
  107.1 94.7 %all-reduce.5.cloned.1.call-start = ((), (), s32[]{:S(2)}) async-start(), calls=%async_computation.5 | async-start | bytes 131072 | tf_op jit(solution)/shard_map/psum | solution.py:142
  113.9 18.5 %copy-start.29 = (f32[256]{0:T(256)}, f32[256]{0:T(256)S(1)}, u32[]{:S(2)}) copy-start(f32[256]{0:T(256)S(1)} %gather_fusion.6) | copy-start | bytes 3076
  127.6 3.1 copy-start
  132.4 3.6 %copy-start.5 = (bf16[4,128,8,128]{1,3,2,0:T(8,128)(2,1)S(1)}, bf16[4,128,8,128]{1,3,2,0:T(8,128)(2,1)}, u32[]{:S(2)}) copy-start(bf16[4,128,8,128]{1,3,2,0:T(8,128)(2,1)} %copy.110) | copy-start | bytes 3145732
  142.1 2.4 copy-start.4
  146.5 2.9 copy-start.1
  146.5 2.9 copy-start.19
  146.5 3.5 %copy-start.6 = (bf16[4,128,8,128]{1,3,2,0:T(8,128)(2,1)S(1)}, bf16[4,128,8,128]{1,3,2,0:T(8,128)(2,1)}, u32[]{:S(2)}) copy-start(bf16[4,128,8,128]{1,3,2,0:T(8,128)(2,1)} %copy.110) | copy-start | bytes 3145732
  146.5 3.5 %copy-start.15 = (f32[4,128,8,128]{1,3,2,0:T(8,128)S(1)}, f32[4,128,8,128]{1,3,2,0:T(8,128)}, u32[]{:S(2)}) copy-start(f32[4,128,8,128]{1,3,2,0:T(8,128)} %copy.113) | copy-start | bytes 6291460
  149.4 1.5 copy-start.9
  158.0 108.7 %all-gather.5.cloned.1.call-start = ((), (), s32[]{:S(2)}) async-start(), calls=%async_computation.6 | async-start | bytes 2621440 | tf_op jit(solution)/shard_map/all_gather | solution.py:171
  166.7 37.5 %copy-start.27 = (bf16[4,128]{1,0:T(4,128)(2,1)}, bf16[4,128]{1,0:T(4,128)(2,1)S(1)}, u32[]{:S(2)}) copy-start(bf16[4,128]{1,0:T(4,128)(2,1)S(1)} %get-tuple-element.4) | copy-start | bytes 3076
  166.7 37.5 %copy-start.33 = (bf16[4,128]{1,0:T(4,128)(2,1)}, bf16[4,128]{1,0:T(4,128)(2,1)S(1)}, u32[]{:S(2)}) copy-start(bf16[4,128]{1,0:T(4,128)(2,1)S(1)} %get-tuple-element.5) | copy-start | bytes 3076
  204.1 1.7 copy-start.21
  204.2 0.8 copy-start.16
  204.2 1.6 copy-start.28
  204.2 1.6 copy-start.34
  204.2 1.6 copy-start.3
  204.2 1.6 copy-start.24
  209.3 2.3 copy-start.18
  211.6 3.3 copy-start.2
  211.6 3.3 copy-start.7
  211.6 3.8 %copy-start.10 = (f32[4,8,128,128]{2,3,1,0:T(8,128)S(1)}, f32[4,8,128,128]{2,3,1,0:T(8,128)}, u32[]{:S(2)}) copy-start(f32[4,8,128,128]{2,3,1,0:T(8,128)} %copy-done.9) | copy-start | bytes 6291460
  211.6 3.8 %copy-start.20 = (f32[4,128,8]{1,2,0:T(8,128)S(1)}, f32[4,128,8]{1,2,0:T(8,128)}, u32[]{:S(2)}) copy-start(f32[4,128,8]{1,2,0:T(8,128)} %copy-done.19) | copy-start | bytes 49156
  214.9 1.6 copy-start.17
  221.4 9.6 %copy-start.37 = (s32[4,64]{1,0:T(4,128)S(1)}, s32[4,64]{1,0:T(4,128)}, u32[]{:S(2)}) copy-start(s32[4,64]{1,0:T(4,128)} %get-tuple-element.17) | copy-start | bytes 3076
  221.4 9.7 %copy-start.35 = (s32[4,127]{1,0:T(4,128)S(1)}, s32[4,127]{1,0:T(4,128)}, u32[]{:S(2)}) copy-start(s32[4,127]{1,0:T(4,128)} %get-tuple-element.13) | copy-start | bytes 6100
  221.4 9.7 %copy-start.36 = (s32[4,1]{1,0:T(4,128)S(1)}, s32[4,1]{1,0:T(4,128)}, u32[]{:S(2)}) copy-start(s32[4,1]{1,0:T(4,128)} %get-tuple-element.15) | copy-start | bytes 52
  231.2 4.3 %copy-start.8 = (bf16[4,128,8,128]{1,3,2,0:T(8,128)(2,1)S(1)}, bf16[4,128,8,128]{1,3,2,0:T(8,128)(2,1)}, u32[]{:S(2)}) copy-start(bf16[4,128,8,128]{1,3,2,0:T(8,128)(2,1)} %copy.110) | copy-start | bytes 3145732
  231.2 4.3 %copy-start.11 = (f32[4,8,128,128]{2,3,1,0:T(8,128)S(1)}, f32[4,8,128,128]{2,3,1,0:T(8,128)}, u32[]{:S(2)}) copy-start(f32[4,8,128,128]{2,3,1,0:T(8,128)} %copy-done.9) | copy-start | bytes 6291460
  231.2 4.3 %copy-start.14 = (bf16[4,128,1024]{1,2,0:T(8,128)(2,1)S(1)}, bf16[4,128,1024]{1,2,0:T(8,128)(2,1)}, u32[]{:S(2)}) copy-start(bf16[4,128,1024]{1,2,0:T(8,128)(2,1)} %copy.130) | copy-start | bytes 3145732
  237.9 3.0 copy-start.38
  237.9 3.1 copy-start.30
  237.9 5.4 %copy-start.22 = (f32[4,128]{1,0:T(4,128)S(1)}, f32[4,128]{1,0:T(4,128)}, u32[]{:S(2)}) copy-start(f32[4,128]{1,0:T(4,128)} %copy-done.21) | copy-start | bytes 6148
  237.9 5.4 %copy-start.25 = (f32[4,128]{1,0:T(4,128)S(1)}, f32[4,128]{1,0:T(4,128)}, u32[]{:S(2)}) copy-start(f32[4,128]{1,0:T(4,128)} %get-tuple-element.23) | copy-start | bytes 6148
  261.0 13.1 %copy-start.12 = (f32[4,128,8,128]{3,2,1,0:T(8,128)S(1)}, f32[4,128,8,128]{3,2,1,0:T(8,128)}, u32[]{:S(2)}) copy-start(f32[4,128,8,128]{3,2,1,0:T(8,128)} %copy.123) | copy-start | bytes 6291460
  274.2 15.6 %copy-start.32 = (f32[256]{0:T(256)S(1)}, f32[256]{0:T(256)}, u32[]{:S(2)}) copy-start(f32[256]{0:T(256)} %copy-done.31) | copy-start | bytes 3076
  281.6 8.2 %copy-start.13 = (f32[256,1024]{1,0:T(8,128)S(1)}, f32[256,1024]{1,0:T(8,128)}, u32[]{:S(2)}) copy-start(f32[256,1024]{1,0:T(8,128)} %scatter_custom_fusion.1) | copy-start | bytes 3145732
  291.7 13.9 %copy-start.23 = (s32[1,64,4]{1,2,0:T(4,128)S(1)}, s32[1,64,4]{1,2,0:T(4,128)}, u32[]{:S(2)}) copy-start(s32[1,64,4]{1,2,0:T(4,128)} %param.9) | copy-start | bytes 3076
  291.7 14.1 %copy-start.40 = (f32[4]{0:T(128)S(1)}, f32[4]{0:T(128)}, u32[]{:S(2)}) copy-start(f32[4]{0:T(128)} %get-tuple-element.12) | copy-start | bytes 52
  291.7 14.1 %copy-start.42 = (s32[4]{0:T(128)S(1)}, s32[4]{0:T(128)}, u32[]{:S(2)}) copy-start(s32[4]{0:T(128)} %param.11) | copy-start | bytes 52
  292.7 30.5 %all-to-all-start.1 = ((bf16[64,4,1024]{2,1,0:T(4,128)(2,1)}), bf16[64,4,1024]{2,1,0:T(4,128)(2,1)S(1)}, u32[]{:S(2)}, u32[]{:S(2)}) async-start(bf16[64,4,1024]{2,1,0:T(4,128)(2,1)} %convert_element_type.151), calls=%async_computation.2 | async-start | bytes 1048576 | tf_op jit(solution)/shard_map/all_to_all | solution.py:182
  (1 other events, 0.7 us)
Sparse Core Ops, SparseCore 0:
  10.7 89.1 all-gather.2
  107.3 28.5 reduce-scatter.1
  158.1 43.6 all-reduce.4
  231.1 35.5 all-gather.4
where the time goes:
time: 339 us; the launch traced here: 333 us
  waiting for transfers between devices  112 us (33%)
  other arithmetic  61.6 us (18%)
  local copies, waits for them, and re-layouts  50 us (15%)
  matrix products  37 us (11%)
  blocking collectives  30.5 us (9%)
  starting transfers between devices  27.5 us (8%)
  between operations  14.6 us (4%)
    all_gather x1, waiting for transfers between devices, local(): lax.all_gather(query_weight, 'sect', axis=1, tiled=True)  34.8 us
    psum x1, waiting for transfers between devices, local(): lax.psum(partial_stats[2].astype(jnp.bfloat16), 'tp').astype(jnp.float32)  34.6 us
    scatter-add x6, other arithmetic, segment_rows(): jax.ops.segment_sum(values.reshape((-1,) + values.shape[2:]), places.resh...  32.6 us
    all_to_all x1, waiting for transfers between devices, local(): lax.all_to_all(outgoing, 'sect', split_axis=0, concat_axis=0, tiled=True)  19.4 us
    all_to_all x1, waiting for transfers between devices, local(): lax.all_to_all(grad_slots.reshape(arrived.shape).astype(jnp.bfloat16), 's...  16.9 us
    all_to_all x1, starting transfers between devices, local(): lax.all_to_all(outgoing, 'sect', split_axis=0, concat_axis=0, tiled=True)  14.3 us
    all_to_all x1, starting transfers between devices, local(): lax.all_to_all(grad_slots.reshape(arrived.shape).astype(jnp.bfloat16), 's...  12.9 us
    unnamed x90, local copies, waits for them, and re-layouts  9.68 us
  transfers between devices with their start and end apart: 6, of which 5 were waited for; matrix products, arithmetic and copies ran while one was open for 20% of the time, Pallas kernels for 0%

commit v1 on v0

--- a/solution.py
+++ b/solution.py
@@ -8,6 +8,13 @@
 CAND = 64
 NORM_FLOOR = 1e-06
 LOGIT_SOFTNESS = 20.0
+
+
+def exchange_gather(array, axis, d):
+    n_dev = lax.axis_size(axis)
+    blocks = jnp.stack([array for _ in range(n_dev)])
+    blocks = lax.all_to_all(blocks, axis, split_axis=0, concat_axis=0)
+    return jnp.concatenate(blocks, axis=d)
 
 
 def head_norm(values, head_count):
@@ -114,9 +121,7 @@
     normed_slots, norm_back = jax.vjp(norm_only, slot_rows, slot_squares)
     normed_low = normed_slots.astype(jnp.bfloat16)
     partial_query = jnp.dot(
-        normed_low,
-        lax.all_gather(query_weight, "sect", axis=1, tiled=True),
-        preferred_element_type=jnp.float32,
+        normed_low, exchange_gather(query_weight, "sect", 1), preferred_element_type=jnp.float32
     )
     query_slots = lax.psum_scatter(
         partial_query.astype(jnp.bfloat16), "tp", scatter_dimension=1, tiled=True

time: 339 us -> 500 us (1.47)
  waiting for transfers between devices: 112 us -> 243 us
  blocking collectives: 30.5 us -> 61.4 us
  starting transfers between devices: 27.5 us -> 19.2 us
    all_to_all x1, waiting for transfers between devices: 19.4 us -> 174 us  [exchange_gather(): blocks = lax.all_to_all(blocks, axis, split_axis=0, concat_axis=0)]
    all_gather x1, waiting for transfers between devices: 34.8 us -> 0.03 us  [local(): lax.all_gather(query_weight, 'sect', axis=1, tiled=True)]
    all_to_all x0 -> x1, blocking collectives: none -> 31.8 us  [local(): lax.all_to_all(outgoing, 'sect', split_axis=0, concat_axis=0, tiled=True)]
    reduce_scatter x1, waiting for transfers between devices: 0.02 us -> 10.3 us  [local(): lax.psum_scatter(partial_query.astype(jnp.bfloat16), 'tp', scatter_dimens...]
    all_to_all x1, starting transfers between devices: 14.3 us -> 6.01 us  [exchange_gather(): blocks = lax.all_to_all(blocks, axis, split_axis=0, concat_axis=0)]
    all_gather x1, waiting for transfers between devices: 5.71 us -> 12.2 us  [local(): lax.all_gather(grad_query_slots.astype(jnp.bfloat16), 'tp', axis=1, tiled...]
    psum x1, waiting for transfers between devices: 34.6 us -> 28.2 us  [local(): lax.psum(partial_stats[2].astype(jnp.bfloat16), 'tp').astype(jnp.float32)]
    unnamed x90 -> x84, local copies, waits for them, and re-layouts: 9.68 us -> 10.6 us
  transfers between devices with their start and end apart: 6 -> 6, of which waited for: 5 -> 5; matrix products, arithmetic and copies ran while one was open for 20% -> 18% of each run, Pallas kernels for 0% -> 0%
where the time goes in v1:
time: 500 us; the launch traced here: 493 us
  waiting for transfers between devices  243 us (49%)
  other arithmetic  61.9 us (12%)
  blocking collectives  61.4 us (12%)
  local copies, waits for them, and re-layouts  54.7 us (11%)
  matrix products  37.1 us (7%)
  starting transfers between devices  19.2 us (4%)
  between operations  16.3 us (3%)
    all_to_all x1, waiting for transfers between devices, exchange_gather(): blocks = lax.all_to_all(blocks, axis, split_axis=0, concat_axis=0)  174 us
    scatter-add x6, other arithmetic, segment_rows(): jax.ops.segment_sum(values.reshape((-1,) + values.shape[2:]), places.resh...  32.6 us
    all_to_all x1, blocking collectives, local(): lax.all_to_all(outgoing, 'sect', split_axis=0, concat_axis=0, tiled=True)  31.8 us
    psum x1, waiting for transfers between devices, local(): lax.psum(partial_stats[2].astype(jnp.bfloat16), 'tp').astype(jnp.float32)  28.2 us
    all_to_all x1, waiting for transfers between devices, local(): lax.all_to_all(grad_slots.reshape(arrived.shape).astype(jnp.bfloat16), 's...  16.9 us
    all_to_all x1, starting transfers between devices, local(): lax.all_to_all(grad_slots.reshape(arrived.shape).astype(jnp.bfloat16), 's...  12.8 us
    all_gather x1, waiting for transfers between devices, local(): lax.all_gather(grad_query_slots.astype(jnp.bfloat16), 'tp', axis=1, tiled...  12.2 us
    unnamed x84, local copies, waits for them, and re-layouts  10.6 us
  transfers between devices with their start and end apart: 6, of which 5 were waited for; matrix products, arithmetic and copies ran while one was open for 18% of the time, Pallas kernels for 0%

profile of v1, /device:TPU:1, one launch (start us, length us, event | category | flops | bytes accessed | tf_op | source)
XLA Modules:
  0.0 493.0 jit_solution(4477898634287077831)
XLA Ops:
  11.3 9.3 %psum.42 = f32[64]{0:T(128)S(1)} all-reduce(f32[64]{0:T(128)S(1)} %fusion.32), channel_id=1, replica_groups=mesh['sect'=64,'tp'=4] {'tp'}, use_global_device_ids=true, to_apply=%region_1.0 | all-reduce | flops 64 | bytes 512 | tf_op jit(solution)/shard_map/psum | solution.py:103
  23.7 31.8 %all_to_all.15 = bf16[64,4,1024]{2,1,0:T(4,128)(2,1)S(1)} all-to-all(bf16[64,4,1024]{2,1,0:T(4,128)(2,1)S(1)} %select_select_fusion), channel_id=1, replica_groups=mesh['sect'=64,'tp'=4] {'sect'}, dimensions={0} | all-to-all | bytes 1048576 | tf_op jit(solution)/shard_map/all_to_all | solution.py:111
  55.5 4.3 stack.2
  59.8 6.0 %all-to-all-start.1 = ((bf16[64,1024,64]{1,2,0:T(8,128)(2,1)}), bf16[64,1024,64]{1,2,0:T(8,128)(2,1)}, u32[]{:S(2)}, u32[]{:S(2)}) async-start(bf16[64,1024,64]{1,2,0:T(8,128)(2,1)} %stack.2), calls=%async_computation.1 | async-start | bytes 16777216 | tf_op jit(solution)/shard_map/all_to_all | solution.py:16
  66.3 6.8 %psum.43 = f32[256]{0:T(256)S(1)} all-reduce(f32[256]{0:T(256)S(1)} %reduce_sum.141), channel_id=1, replica_groups=mesh['sect'=64,'tp'=4] {'tp'}, use_global_device_ids=true, to_apply=%region_3.4 | all-reduce | flops 256 | bytes 2048 | tf_op jit(solution)/shard_map/psum | solution.py:115
  73.7 174.4 %all-to-all-done.1 = bf16[64,1024,64]{1,2,0:T(8,128)(2,1)} async-done(((bf16[64,1024,64]{1,2,0:T(8,128)(2,1)}), bf16[64,1024,64]{1,2,0:T(8,128)(2,1)}, u32[]{:S(2)}, u32[]{:S(2)}) %all-to-all-start.1) | async-done | bytes 8388640 | tf_op jit(solution)/shard_map/all_to_all | solution.py:16
  248.1 7.1 %convolution_convert_fusion = bf16[256,4096]{1,0:T(8,128)(2,1)} fusion(bf16[256,1024]{1,0:T(8,128)(2,1)S(1)} %convert_element_type.131, bf16[1024,4096]{0,1:T(8,128)(2,1)} %bitcast.7), kind=kOutput, calls=%fused_computation.14 | convolution fusion | flops 2148532224 | bytes 11010048 | tf_op jit(solution)/shard_map/dot_general | solution.py:123
  257.9 2.1 gather_fusion.2
  261.2 2.4 copy.111
  263.7 2.7 gather_fusion.1
  266.4 3.4 copy.134
  269.8 3.1 copy.114
  275.9 10.3 %reduce-scatter.2.cloned.1.call-done = bf16[256,1024]{1,0:T(8,128)(2,1)} async-done(((bf16[256,4096]{1,0:T(8,128)(2,1)}), bf16[256,1024]{1,0:T(8,128)(2,1)}) %reduce-scatter.2.cloned.1.call-update) | async-done | bytes 524304 | tf_op jit(solution)/shard_map/reduce_scatter | solution.py:126
  287.3 2.7 gather_fusion.3
  290.0 2.1 copy.133
  294.5 1.9 copy.107
  296.5 2.8 fusion.20
  300.8 1.8 copy.113
  302.6 3.2 multiply_reduce_fusion
  305.8 2.0 convolution_convert_fusion.5
  309.7 1.9 gather_fusion.6
  312.4 3.5 gather_fusion.4
  315.9 6.8 %all-reduce.2 = (bf16[4,128]{1,0:T(4,128)(2,1)S(1)}, bf16[4,128]{1,0:T(4,128)(2,1)S(1)}) all-reduce(bf16[4,128]{1,0:T(4,128)(2,1)S(1)} %get-tuple-element.27, bf16[4,128]{1,0:T(4,128)(2,1)S(1)} %get-tuple-element.10), channel_id=1, replica_groups=mesh['sect'=64,'tp'=4] {'tp'}, use_global_device_ids=true, to_apply=%region_11.12 | all-reduce | flops 1024 | bytes 4096 | tf_op jit(solution)/shard_map/psum | solution.py:145
  323.9 28.2 %all-reduce.5.cloned.1.call-done = bf16[4,128,64]{1,2,0:T(8,128)(2,1)} async-done(((bf16[4,128,64]{1,2,0:T(8,128)(2,1)}), bf16[4,128,64]{1,2,0:T(8,128)(2,1)}) %all-reduce.5.cloned.1.call-update) | async-done | bytes 65552 | tf_op jit(solution)/shard_map/psum | solution.py:147
  354.3 1.6 fusion.43
  357.6 3.5 pad_add_fusion
  361.1 2.3 copy.131
  363.4 3.3 fusion.5
  368.5 1.9 add_add_fusion.1
  370.4 2.9 copy.121
  373.3 7.5 %scatter_custom_fusion.2 = f32[256,1024]{1,0:T(8,128)} fusion(s32[512]{0:T(512)} %get-tuple-element.20, f32[64,8,8,128]{3,2,1,0:T(8,128)} %bitcast.117, f32[]{:T(128)} %constant.17.clone.1), kind=kCustom, calls=%fused_computation.37 | custom fusion | flops 524288 | bytes 3146240 | tf_op jit(solution)/shard_map/scatter-add | solution.py:96
  380.8 2.1 convert_element_type.151
  383.1 4.4 fusion.9
  387.6 2.4 fusion.6
  390.0 3.0 copy.124
  393.1 2.3 scatter_custom_fusion.5
  395.4 2.3 fusion.46
  397.7 4.3 scatter_custom_fusion.1
  402.0 6.8 %scatter_custom_fusion = f32[256,1024]{1,0:T(8,128)} fusion(s32[512]{0:T(512)} %get-tuple-element.20, f32[512,1024]{1,0:T(8,128)} %bitcast.126, f32[]{:T(128)} %constant.17.clone.1), kind=kCustom, calls=%fused_computation.74 | custom fusion | flops 524288 | bytes 1049088 | tf_op jit(solution)/shard_map/scatter-add | solution.py:96
  408.8 4.2 scatter_custom_fusion.4
  413.1 12.2 %all-gather.3.cloned.1.call-done = bf16[256,4096]{1,0:T(8,128)(2,1)} async-done(((bf16[256,1024]{1,0:T(8,128)(2,1)}), bf16[256,4096]{1,0:T(8,128)(2,1)}) %all-gather.3.cloned.1.call-update) | async-done | bytes 2097168 | tf_op jit(solution)/shard_map/all_gather | solution.py:176
  425.3 7.4 %fusion.81 = f32[256,1024]{1,0:T(8,128)} fusion(bf16[256,4096]{1,0:T(8,128)(2,1)} %all-gather.3.cloned.1.call-done, bf16[1024,4096]{0,1:T(8,128)(2,1)} %all-gather.5.cloned.1.call-done), kind=kOutput, calls=%fused_computation.176 | convolution fusion | flops 2147483648 | bytes 11534336 | tf_op jit(solution)/shard_map/dot_general | solution.py:177
  432.7 7.4 %scatter_custom_fusion.3 = f32[256,1024]{1,0:T(8,128)} fusion(f32[256,1024]{1,0:T(8,128)} %fusion.81, s32[512]{0:T(512)} %get-tuple-element.20, f32[64,8,8,128]{3,2,1,0:T(8,128)S(1)} %bitcast.116), kind=kCustom, calls=%fused_computation.34 | custom fusion | flops 524288 | bytes 3145728 | tf_op jit(solution)/shard_map/scatter-add | solution.py:96
  441.7 6.7 %psum.47 = f32[256]{0:T(256)S(1)} all-reduce(f32[256]{0:T(256)S(1)} %multiply_multiply_fusion.7), channel_id=1, replica_groups=mesh['sect'=64,'tp'=4] {'tp'}, use_global_device_ids=true, to_apply=%region_26.27 | all-reduce | flops 256 | bytes 2048 | tf_op jit(solution)/shard_map/psum | solution.py:185
  448.4 2.0 add_convert_fusion
  451.4 12.8 %all-to-all-start.2 = ((bf16[64,4,1024]{2,1,0:T(4,128)(2,1)}), bf16[64,4,1024]{2,1,0:T(4,128)(2,1)S(1)}, u32[]{:S(2)}, u32[]{:S(2)}) async-start(bf16[64,4,1024]{2,1,0:T(4,128)(2,1)} %convert_element_type.159), calls=%async_computation.3 | async-start | bytes 1048576 | tf_op jit(solution)/shard_map/all_to_all | solution.py:187
  465.0 16.9 %all-to-all-done.2 = bf16[64,4,1024]{2,1,0:T(4,128)(2,1)S(1)} async-done(((bf16[64,4,1024]{2,1,0:T(4,128)(2,1)}), bf16[64,4,1024]{2,1,0:T(4,128)(2,1)S(1)}, u32[]{:S(2)}, u32[]{:S(2)}) %all-to-all-start.2) | async-done | bytes 524320 | tf_op jit(solution)/shard_map/all_to_all | solution.py:187
  482.0 2.7 scatter_custom_fusion.6
  (163 shorter events, 33.2 us)
Async XLA Ops:
  23.0 32.5 %copy-start.18 = (bf16[1024,64]{0,1:T(8,128)(2,1)S(1)}, bf16[1024,64]{0,1:T(8,128)(2,1)}, u32[]{:S(2)}) copy-start(bf16[1024,64]{0,1:T(8,128)(2,1)} %param.13) | copy-start | bytes 393220
  59.8 6.1 %copy-start.36 = (bf16[1024]{0:T(1024)(128)(2,1)S(1)}, bf16[1024]{0:T(1024)(128)(2,1)}, u32[]{:S(2)}) copy-start(bf16[1024]{0:T(1024)(128)(2,1)} %param.12) | copy-start | bytes 6148
  59.8 188.3 %all-to-all-start.1 = ((bf16[64,1024,64]{1,2,0:T(8,128)(2,1)}), bf16[64,1024,64]{1,2,0:T(8,128)(2,1)}, u32[]{:S(2)}, u32[]{:S(2)}) async-start(bf16[64,1024,64]{1,2,0:T(8,128)(2,1)} %stack.2), calls=%async_computation.1 | async-start | bytes 16777216 | tf_op jit(solution)/shard_map/all_to_all | solution.py:16
  65.8 220.3 %reduce-scatter.2.cloned.1.call-start = ((), (), s32[]{:S(2)}) async-start(), calls=%async_computation.4 | async-start | bytes 2621440 | tf_op jit(solution)/shard_map/reduce_scatter | solution.py:126
  73.2 184.5 %copy-start.27 = (f32[256]{0:T(256)}, f32[256]{0:T(256)S(1)}, u32[]{:S(2)}) copy-start(f32[256]{0:T(256)S(1)} %fusion.68) | copy-start | bytes 3076
  255.3 0.7 copy-start.29
  255.3 2.0 copy-start.38
  255.3 96.8 %all-reduce.5.cloned.1.call-start = ((), (), s32[]{:S(2)}) async-start(), calls=%async_computation.5 | async-start | bytes 131072 | tf_op jit(solution)/shard_map/psum | solution.py:147
  269.8 3.1 copy-start
  274.4 1.2 copy-start.5
  292.1 2.4 copy-start.4
  296.5 2.9 copy-start.1
  296.5 2.9 copy-start.20
  296.5 2.9 copy-start.6
  296.5 3.0 copy-start.15
  299.4 1.4 copy-start.9
  307.8 105.3 %all-gather.5.cloned.1.call-start = ((), (), s32[]{:S(2)}) async-start(), calls=%async_computation.7 | async-start | bytes 8519680 | tf_op jit(solution)/shard_map/all_gather | solution.py:179
  308.4 116.9 %all-gather.3.cloned.1.call-start = ((), (), s32[]{:S(2)}) async-start(), calls=%async_computation.6 | async-start | bytes 2621440 | tf_op jit(solution)/shard_map/all_gather | solution.py:176
  311.7 0.6 copy-start.30
  354.3 1.9 copy-start.22
  356.0 1.6 copy-start.3
  356.0 1.6 copy-start.16
  356.0 1.6 copy-start.25
  361.1 2.3 copy-start.19
  363.4 3.3 copy-start.2
  363.4 3.3 copy-start.7
  363.4 4.0 copy-start.10
  363.4 4.0 copy-start.21
  366.7 1.8 copy-start.17
  373.3 9.7 %copy-start.34 = (s32[4,64]{1,0:T(4,128)S(1)}, s32[4,64]{1,0:T(4,128)}, u32[]{:S(2)}) copy-start(s32[4,64]{1,0:T(4,128)} %get-tuple-element.17) | copy-start | bytes 3076
  373.3 9.8 %copy-start.32 = (s32[4,127]{1,0:T(4,128)S(1)}, s32[4,127]{1,0:T(4,128)}, u32[]{:S(2)}) copy-start(s32[4,127]{1,0:T(4,128)} %get-tuple-element.13) | copy-start | bytes 6100
  373.3 9.8 %copy-start.33 = (s32[4,1]{1,0:T(4,128)S(1)}, s32[4,1]{1,0:T(4,128)}, u32[]{:S(2)}) copy-start(s32[4,1]{1,0:T(4,128)} %get-tuple-element.15) | copy-start | bytes 52
  383.1 4.5 copy-start.8
  383.1 4.5 copy-start.11
  383.1 4.5 copy-start.14
  390.0 3.0 copy-start.35
  390.0 3.1 copy-start.31
  390.0 5.4 %copy-start.23 = (f32[4,128]{1,0:T(4,128)S(1)}, f32[4,128]{1,0:T(4,128)}, u32[]{:S(2)}) copy-start(f32[4,128]{1,0:T(4,128)} %copy-done.22) | copy-start | bytes 6148
  390.0 5.4 %copy-start.26 = (f32[4,128]{1,0:T(4,128)S(1)}, f32[4,128]{1,0:T(4,128)}, u32[]{:S(2)}) copy-start(f32[4,128]{1,0:T(4,128)} %get-tuple-element.23) | copy-start | bytes 6148
  413.1 19.6 %copy-start.12 = (f32[4,128,8,128]{3,2,1,0:T(8,128)S(1)}, f32[4,128,8,128]{3,2,1,0:T(8,128)}, u32[]{:S(2)}) copy-start(f32[4,128,8,128]{3,2,1,0:T(8,128)} %copy.124) | copy-start | bytes 6291460
  432.7 15.6 %copy-start.28 = (f32[256]{0:T(256)S(1)}, f32[256]{0:T(256)}, u32[]{:S(2)}) copy-start(f32[256]{0:T(256)} %copy-done.27) | copy-start | bytes 3076
  440.1 8.2 %copy-start.13 = (f32[256,1024]{1,0:T(8,128)S(1)}, f32[256,1024]{1,0:T(8,128)}, u32[]{:S(2)}) copy-start(f32[256,1024]{1,0:T(8,128)} %scatter_custom_fusion.1) | copy-start | bytes 3145732
  450.3 13.9 %copy-start.24 = (s32[1,64,4]{1,2,0:T(4,128)S(1)}, s32[1,64,4]{1,2,0:T(4,128)}, u32[]{:S(2)}) copy-start(s32[1,64,4]{1,2,0:T(4,128)} %param.9) | copy-start | bytes 3076
  450.3 14.1 %copy-start.37 = (f32[4]{0:T(128)S(1)}, f32[4]{0:T(128)}, u32[]{:S(2)}) copy-start(f32[4]{0:T(128)} %get-tuple-element.12) | copy-start | bytes 52
  450.4 14.1 %copy-start.39 = (s32[4]{0:T(128)S(1)}, s32[4]{0:T(128)}, u32[]{:S(2)}) copy-start(s32[4]{0:T(128)} %param.11) | copy-start | bytes 52
  451.4 30.5 %all-to-all-start.2 = ((bf16[64,4,1024]{2,1,0:T(4,128)(2,1)}), bf16[64,4,1024]{2,1,0:T(4,128)(2,1)S(1)}, u32[]{:S(2)}, u32[]{:S(2)}) async-start(bf16[64,4,1024]{2,1,0:T(4,128)(2,1)} %convert_element_type.159), calls=%async_computation.3 | async-start | bytes 1048576 | tf_op jit(solution)/shard_map/all_to_all | solution.py:187
Sparse Core Ops, SparseCore 0:
  255.4 30.7 reduce-scatter.1
  307.9 44.0 all-reduce.4
Sparse Core Ops, SparseCore 1:
  311.0 83.3 all-gather.4
  396.0 29.2 all-gather.2
